TPU v7x, 32 devices: a whole 2x2x4 slice. The times are simulated.
32 devices in a mesh: wide: 16 (over z, x, core), narrow: 2 (over y).
Axes of the slice: x: 2, y: 2, z: 4, core: 2. Of those that a mesh axis runs over, the one named last changes fastest.
Arguments:
- hidden: bfloat16 [128, 16384], P('wide', 'narrow'), may hold values from -6 to 6
- down_weight: bfloat16 [16384, 4096], P(('wide', 'narrow')), may hold values from -0.046875 to 0.046875
- rotation: float32 [4096, 4096], P('wide', 'narrow'), may hold values from -1 to 1, as said below
- cotangent: bfloat16 [128, 4096], P('wide', 'narrow'), may hold values from -6 to 6
- token_exps: int32 [128], P('wide'), may hold values from -2 to 0
- column_exps: int32 [4096], P('narrow'), may hold values from -9 to -7
- sign_bits: int32 [16384], P('narrow'), may hold values 0 or 1
- step_size: float32 [], replicated, may hold values from 0.00015 to 0.0003
Outputs:
- projected: bfloat16 [128, 4096], P('wide', 'narrow')
- new_rotation: float32 [4096, 4096], P('wide', 'narrow')
Inputs may be any that keep to these rules, and one draw needn't show every extreme that they name: `rotation`: an orthogonal matrix up to float32 rounding.
All inputs are finite; a program needn't handle non-finite values. No bound on the sum of `sign_bits` on one device may be relied on, other than what follows from the above.
Results may differ from a plain program's by a relative error of at most 0.003.
The roundings to bfloat16 on the way count: a program that leaves them out, or rounds other values in their place, can miss the bound.
Values may be sent and summed in bfloat16 or wider, within the bound.
No kernel may reach another device: no remote copies, remote signals or barrier semaphores. Data moves between devices by JAX's collectives and lax.ppermute only.
A program may use at most 128 MiB of HBM per device.

v0:
```python
import math
import jax
import jax.numpy as jnp
from jax import lax
from jax.sharding import PartitionSpec as P

D = 4096
FF = 16384
HIGHEST_PREC = lax.Precision.HIGHEST
LEVELS = 7.0
TWO_PI = 2.0 * math.pi


def sylvester(length):
    positions = jnp.arange(length, dtype=jnp.int32)
    common = jnp.bitwise_and(positions[:, None], positions[None, :])
    parity = jnp.zeros((length, length), jnp.int32)
    for offset in range(max(length.bit_length() - 1, 0)):
        parity = parity + jnp.bitwise_and(jnp.right_shift(common, offset), 1)
    return (1 - 2 * (parity % 2)).astype(jnp.float32)


def local_hadamard(values):
    row_count, length = values.shape
    inner_size = min(length, 128)
    outer_size = length // inner_size
    blocks = values.reshape(row_count, outer_size, inner_size)
    blocks = jnp.einsum("rab,bc->rac", blocks, sylvester(inner_size), precision=HIGHEST_PREC)
    blocks = jnp.einsum("rab,ac->rcb", blocks, sylvester(outer_size), precision=HIGHEST_PREC)
    return blocks.reshape(row_count, length)


def fake_quant(values, exponents):
    scales = jnp.exp2(exponents.astype(jnp.float32))
    clipped = LEVELS * jnp.tanh(values / scales / LEVELS)
    return scales * (clipped - jnp.sin(TWO_PI * clipped) / TWO_PI)


def inner_rows(left, right):
    return lax.dot_general(left, right, (((0,), (0,)), ((), ())), precision=HIGHEST_PREC)


def on_device(
    hidden, down_weight, rotation, cotangent, token_exps, column_exps, sign_bits, step_size
):
    narrow_count = lax.axis_size("narrow")
    sign_flip = (1 - 2 * sign_bits).astype(jnp.float32)
    partial_mix = local_hadamard(hidden.astype(jnp.float32) * sign_flip[None, :])
    joined = lax.all_gather(partial_mix, "narrow", axis=1, tiled=True)
    row_count = joined.shape[0]
    stacked = joined.reshape(row_count, narrow_count, -1)
    stacked = jnp.einsum("rnf,nm->rmf", stacked, sylvester(narrow_count), precision=HIGHEST_PREC)
    rotated = stacked.reshape(row_count, -1) / math.sqrt(FF)
    token_block = fake_quant(rotated, token_exps[:, None]).astype(jnp.bfloat16)
    quantized = lax.all_to_all(token_block, "wide", split_axis=1, concat_axis=0, tiled=True)
    weight_panel = lax.all_gather(down_weight, "narrow", axis=0, tiled=True)
    rot_half = rotation.astype(jnp.bfloat16)
    col_width = rotation.shape[1]
    weight_rot = jnp.dot(
        weight_panel,
        lax.all_gather(rot_half, "wide", axis=0, tiled=True),
        preferred_element_type=jnp.float32,
    )
    weight_quant = fake_quant(weight_rot, column_exps[None, :]).astype(jnp.bfloat16)
    col_start = lax.axis_index("narrow") * col_width
    weight_local = lax.dynamic_slice_in_dim(weight_panel, col_start, col_width, 1)
    both_weights = jnp.concatenate([weight_quant, weight_local], axis=1)
    summed = lax.psum_scatter(
        jnp.dot(quantized, both_weights, preferred_element_type=jnp.float32),
        "wide",
        scatter_dimension=0,
        tiled=True,
    )
    projected = summed[:, :col_width].astype(jnp.bfloat16)
    unrotated = summed[:, col_width:].astype(jnp.bfloat16)
    target_rows = lax.all_gather(cotangent, "wide", axis=0, tiled=True)
    mixed_wide = lax.all_gather(unrotated, "narrow", axis=1, tiled=True)
    mixed_cols = lax.all_to_all(mixed_wide, "wide", split_axis=1, concat_axis=0, tiled=True)
    gradient = lax.dot_general(
        mixed_cols, target_rows, (((0,), (0,)), ((), ())), preferred_element_type=jnp.float32
    )
    target_wide = target_rows.astype(jnp.float32)
    part_proj = jnp.dot(target_wide, rotation.T, precision=HIGHEST_PREC)
    projection = lax.psum(part_proj.astype(jnp.bfloat16), "narrow").astype(jnp.float32)
    factors = jnp.concatenate([mixed_cols.astype(jnp.float32), projection], axis=0)
    token_count = mixed_cols.shape[0]
    current = rotation - step_size * gradient
    applied = lax.psum(jnp.dot(factors, rotation + current, precision=HIGHEST_PREC), "wide")
    turned = inner_rows(factors[:token_count], applied[token_count:]) - inner_rows(
        factors[token_count:], applied[:token_count]
    )
    current = rotation - 0.5 * step_size * turned
    return (projected, math.sqrt(D) * current)


def solution(mesh):
    in_specs = (
        P("wide", "narrow"),
        P(("wide", "narrow"), None),
        P("wide", "narrow"),
        P("wide", "narrow"),
        P("wide"),
        P("narrow"),
        P("narrow"),
        P(),
    )
    out_specs = (P("wide", "narrow"), P("wide", "narrow"))
    return jax.shard_map(
        on_device, mesh=mesh, in_specs=in_specs, out_specs=out_specs, check_vma=False
    )
```

profile of v0, /device:TPU:0, one launch (start us, length us, event | category | flops | bytes accessed | tf_op | source)
XLA Modules:
  0.0 513.1 jit_solution(12951212293462382946)
XLA Ops:
  7.2 0.0 copy-start
  7.2 0.0 copy-start.4
  7.2 0.0 copy-start.2
  7.2 0.0 all-gather.3.cloned.1.call-start
  7.2 0.7 all-gather.3.cloned.1.call-update
  7.9 0.0 all-gather.5.cloned.1.call-start
  8.0 0.8 copy-done
  8.8 1.1 convert_element_type.49
  9.9 0.0 copy-start.6
  9.9 0.0 copy-start.5
  9.9 0.0 all-gather.5.cloned.1.call-update
  9.9 0.0 copy-done.4
  9.9 0.0 copy-done.2
  10.0 0.4 fusion.14
  10.4 0.4 convolution_bitcast_fusion
  10.8 0.2 copy.23
  11.0 10.0 %all_gather.15 = f32[8,16384]{1,0:T(8,128)S(1)} all-gather(f32[8,8192]{1,0:T(8,128)S(1)} %bitcast.42), channel_id=1, replica_groups=mesh['wide'=16,'narrow'=2] {'narrow'}, dimensions={1}, use_global_device_ids=true | all-gather | bytes 786432 | tf_op jit(solution)/shard_map/all_gather | solution.py:49
  20.9 0.5 reshape.43
  21.4 2.7 fusion
  24.1 1.6 div.38
  25.7 0.0 copy-done.6
  25.7 2.8 multiply_convert_fusion.1
  28.5 6.1 %all-to-all-start = ((bf16[8,16,1024]{2,0,1:T(8,128)(2,1)}), bf16[8,16,1024]{2,0,1:T(8,128)(2,1)S(1)}, u32[]{:S(2)}, u32[]{:S(2)}) async-start(bf16[8,16,1024]{2,0,1:T(8,128)(2,1)} %multiply_convert_fusion.1), calls=%async_computation | async-start | bytes 524288 | tf_op jit(solution)/shard_map/all_to_all | solution.py:55
  34.6 0.2 reduce-scatter.2.cloned.1.call-start
  34.9 0.0 copy-done.5
  34.9 81.4 %all-gather.3.cloned.1.call-done = bf16[1024,4096]{1,0:T(8,128)(2,1)} async-done(((bf16[512,4096]{1,0:T(8,128)(2,1)}), bf16[1024,4096]{1,0:T(8,128)(2,1)}) %all-gather.3.cloned.1.call-update) | async-done | bytes 8388624 | tf_op jit(solution)/shard_map/all_gather | solution.py:56
  116.3 4.7 constant_dynamic-slice_fusion
  121.0 124.5 %all-gather.5.cloned.1.call-done = bf16[4096,2048]{1,0:T(8,128)(2,1)} async-done(((bf16[256,2048]{1,0:T(8,128)(2,1)}), bf16[4096,2048]{1,0:T(8,128)(2,1)}) %all-gather.5.cloned.1.call-update) | async-done | bytes 16777232 | tf_op jit(solution)/shard_map/all_gather | solution.py:61
  245.5 51.8 %multiply_convert_fusion = bf16[1024,2048]{1,0:T(8,128)(2,1)} fusion(bf16[1024,4096]{1,0:T(8,128)(2,1)} %all-gather.3.cloned.1.call-done, bf16[4096,2048]{1,0:T(8,128)(2,1)} %all-gather.5.cloned.1.call-done, f32[2048]{0:T(1024)S(1)} %multiply_exponential_fusion), kind=kOutput, calls=%fused_computation.6 | convolution fusion | flops 17196646400 | bytes 29368320 | tf_op jit(solution)/shard_map/dot_general | solution.py:59
  297.2 0.0 copy-start.3
  297.2 0.0 all-to-all-done
  297.2 5.5 %fusion.1 = f32[128,4096]{1,0:T(8,128)} fusion(bf16[1024,2048]{1,0:T(8,128)(2,1)} %constant_dynamic-slice_fusion, bf16[1024,2048]{1,0:T(8,128)(2,1)} %multiply_convert_fusion, bf16[8,16,1024]{2,0,1:T(8,128)(2,1)S(1)} %all-to-all-done), kind=kOutput, calls=%fused_computation.2 | convolution fusion | flops 1090519040 | bytes 10747904 | tf_op jit(solution)/shard_map/dot_general | solution.py:69
  302.8 0.0 reduce-scatter.2.cloned.1.call-update
  302.8 0.0 copy-done.3
  302.8 19.9 %all_gather.19 = bf16[128,2048]{1,0:T(8,128)(2,1)S(1)} all-gather(bf16[8,2048]{1,0:T(8,128)(2,1)S(1)} %copy-done.3), channel_id=1, replica_groups=mesh['wide'=16,'narrow'=2] {'wide'}, dimensions={0}, use_global_device_ids=true | all-gather | bytes 557056 | tf_op jit(solution)/shard_map/all_gather | solution.py:76
  322.7 40.3 %reduce-scatter.2.cloned.1.call-done = f32[8,4096]{1,0:T(8,128)} async-done(((f32[128,4096]{1,0:T(8,128)}), f32[8,4096]{1,0:T(8,128)}) %reduce-scatter.2.cloned.1.call-update) | async-done | bytes 131088 | tf_op jit(solution)/shard_map/reduce_scatter | solution.py:68
  362.9 0.9 convert.5
  363.9 0.6 fusion.85
  364.5 4.7 all_gather.18
  369.2 3.7 all-to-all-start.1
  372.8 0.3 all-reduce.3.cloned.1.call-start
  373.1 1.9 convolution_convert_fusion
  375.0 0.0 all-reduce.3.cloned.1.call-update
  375.0 0.0 all-reduce.5.cloned.1.call-start
  375.7 4.0 all-to-all-done.1
  379.7 1.8 subtract_add_fusion
  381.5 16.3 %all-reduce.3.cloned.1.call-done = bf16[128,256]{1,0:T(8,128)(2,1)} async-done(((bf16[128,256]{1,0:T(8,128)(2,1)}), bf16[128,256]{1,0:T(8,128)(2,1)}) %all-reduce.3.cloned.1.call-update) | async-done | bytes 65552 | tf_op jit(solution)/shard_map/psum | solution.py:84
  397.8 0.0 copy-start.1
  397.8 4.2 fusion.16
  402.0 0.0 all-reduce.5.cloned.1.call-update
  402.0 98.3 %all-reduce.5.cloned.1.call-done = f32[256,2048]{1,0:T(8,128)} async-done(((f32[256,2048]{1,0:T(8,128)}), f32[256,2048]{1,0:T(8,128)}) %all-reduce.5.cloned.1.call-update) | async-done | bytes 2097168 | tf_op jit(solution)/shard_map/psum | solution.py:88
  500.3 2.2 fusion.9
  502.6 0.0 copy-done.1
  502.6 3.9 fusion.7
  (4 shorter events, 0.0 us)
Async XLA Ops:
  7.2 1.6 copy-start
  7.2 2.7 copy-start.4
  7.2 2.8 copy-start.2
  7.2 109.1 %all-gather.3.cloned.1.call-start = ((), (), s32[]{:S(2)}) async-start(), calls=%async_computation.3 | async-start | bytes 12582912 | tf_op jit(solution)/shard_map/all_gather | solution.py:56
  7.9 237.5 %all-gather.5.cloned.1.call-start = ((), (), s32[]{:S(2)}) async-start(), calls=%async_computation.4 | async-start | bytes 17825792 | tf_op jit(solution)/shard_map/all_gather | solution.py:61
  9.9 15.8 %copy-start.6 = (s32[8]{0:T(128)S(1)}, s32[8]{0:T(128)}, u32[]{:S(2)}) copy-start(s32[8]{0:T(128)} %param.12) | copy-start | bytes 100
  9.9 25.0 %copy-start.5 = (s32[2048]{0:T(1024)S(1)}, s32[2048]{0:T(1024)}, u32[]{:S(2)}) copy-start(s32[2048]{0:T(1024)} %param.13) | copy-start | bytes 24580
  28.5 268.8 %all-to-all-start = ((bf16[8,16,1024]{2,0,1:T(8,128)(2,1)}), bf16[8,16,1024]{2,0,1:T(8,128)(2,1)S(1)}, u32[]{:S(2)}, u32[]{:S(2)}) async-start(bf16[8,16,1024]{2,0,1:T(8,128)(2,1)} %multiply_convert_fusion.1), calls=%async_computation | async-start | bytes 524288 | tf_op jit(solution)/shard_map/all_to_all | solution.py:55
  34.6 328.3 %reduce-scatter.2.cloned.1.call-start = ((), (), s32[]{:S(2)}) async-start(), calls=%async_computation.5 | async-start | bytes 2228224 | tf_op jit(solution)/shard_map/reduce_scatter | solution.py:68
  297.2 5.6 %copy-start.3 = (bf16[8,2048]{1,0:T(8,128)(2,1)S(1)}, bf16[8,2048]{1,0:T(8,128)(2,1)}, u32[]{:S(2)}) copy-start(bf16[8,2048]{1,0:T(8,128)(2,1)} %param.11) | copy-start | bytes 98308
  369.2 10.6 %all-to-all-start.1 = ((bf16[8,16,256]{2,0,1:T(8,128)(2,1)}), bf16[8,16,256]{2,0,1:T(8,128)(2,1)S(1)}, u32[]{:S(2)}, u32[]{:S(2)}) async-start(bf16[8,16,256]{2,0,1:T(8,128)(2,1)} %bitcast.8), calls=%async_computation.2 | async-start | bytes 131072 | tf_op jit(solution)/shard_map/all_to_all | solution.py:78
  372.8 25.0 %all-reduce.3.cloned.1.call-start = ((), (), s32[]{:S(2)}) async-start(), calls=%async_computation.6 | async-start | bytes 131072 | tf_op jit(solution)/shard_map/psum | solution.py:84
  375.0 125.3 %all-reduce.5.cloned.1.call-start = ((), (), s32[]{:S(2)}) async-start(), calls=%async_computation.7 | async-start | bytes 4194304 | tf_op jit(solution)/shard_map/psum | solution.py:88
  397.8 104.8 %copy-start.1 = (bf16[128,256]{1,0:T(8,128)(2,1)S(1)}, bf16[128,256]{1,0:T(8,128)(2,1)}, u32[]{:S(2)}) copy-start(bf16[128,256]{1,0:T(8,128)(2,1)} %all-reduce.3.cloned.1.call-done) | copy-start | bytes 196612
Sparse Core Ops, SparseCore 0:
  9.5 106.6 all-gather.2
  119.0 126.4 all-gather.4
  302.9 59.9 reduce-scatter.1
  375.6 22.2 all-reduce.2
  402.2 98.1 all-reduce.4
where the time goes:
time: 514 us; the launch traced here: 513 us
  waiting for transfers between devices  365 us (71%)
  matrix products  74.8 us (15%)
  blocking collectives  34.5 us (7%)
  between operations  14.6 us (3%)
  starting transfers between devices  10.4 us (2%)
  local copies, waits for them, and re-layouts  8.37 us (2%)
    all_gather x1, waiting for transfers between devices, on_device(): lax.all_gather(rot_half, 'wide', axis=0, tiled=True)  124 us
    psum x1, waiting for transfers between devices, on_device(): lax.psum(jnp.dot(factors, rotation + current, precision=HIGHEST_PREC), 'w...  98.3 us
    all_gather x1, waiting for transfers between devices, on_device(): weight_panel = lax.all_gather(down_weight, 'narrow', axis=0, tiled=True)  81.4 us
    dot_general x1, matrix products, on_device(): jnp.dot(weight_panel, lax.all_gather(rot_half, 'wide', axis=0, tiled=True...  51.8 us
    reduce_scatter x1, waiting for transfers between devices, on_device(): lax.psum_scatter(jnp.dot(quantized, both_weights, preferred_element_type=...  40.3 us
    all_gather x1, blocking collectives, on_device(): target_rows = lax.all_gather(cotangent, 'wide', axis=0, tiled=True)  19.9 us
    psum x1, waiting for transfers between devices, on_device(): lax.psum(part_proj.astype(jnp.bfloat16), 'narrow').astype(jnp.float32)  16.3 us
  transfers between devices with their start and end apart: 7, of which 6 were waited for; matrix products, arithmetic and copies ran while one was open for 14% of the time, Pallas kernels for 0%

commit v1 on v0

--- a/solution.py
+++ b/solution.py
@@ -85,7 +85,9 @@
     factors = jnp.concatenate([mixed_cols.astype(jnp.float32), projection], axis=0)
     token_count = mixed_cols.shape[0]
     current = rotation - step_size * gradient
-    applied = lax.psum(jnp.dot(factors, rotation + current, precision=HIGHEST_PREC), "wide")
+    x = jnp.dot(factors, rotation + current, precision=HIGHEST_PREC)
+    shards = lax.all_gather(x, "wide", axis=0, tiled=False)
+    applied = shards.sum(axis=0)
     turned = inner_rows(factors[:token_count], applied[token_count:]) - inner_rows(
         factors[token_count:], applied[:token_count]
     )

time: 514 us -> 597 us (1.16)
  waiting for transfers between devices: 365 us -> 435 us
  other arithmetic: 4.87 us -> 18 us
    all_gather x0 -> x1, waiting for transfers between devices: none -> 168 us  [on_device(): shards = lax.all_gather(x, 'wide', axis=0, tiled=False)]
    psum x1 -> x0, waiting for transfers between devices: 98.3 us -> none  [on_device(): lax.psum(jnp.dot(factors, rotation + current, precision=HIGHEST_PREC), 'w...]
    reduce_sum x0 -> x1, other arithmetic: none -> 13.1 us  [on_device(): applied = shards.sum(axis=0)]
  transfers between devices with their start and end apart: 7 -> 7, of which waited for: 6 -> 6; matrix products, arithmetic and copies ran while one was open for 14% -> 12% of each run, Pallas kernels for 0% -> 0%
where the time goes in v1:
time: 597 us; the launch traced here: 596 us
  waiting for transfers between devices  435 us (73%)
  matrix products  74.7 us (13%)
  blocking collectives  34.5 us (6%)
  other arithmetic  18 us (3%)
  between operations  14.6 us (2%)
  starting transfers between devices  10.4 us (2%)
  local copies, waits for them, and re-layouts  8.37 us (1%)
    all_gather x1, waiting for transfers between devices, on_device(): shards = lax.all_gather(x, 'wide', axis=0, tiled=False)  168 us
    all_gather x1, waiting for transfers between devices, on_device(): lax.all_gather(rot_half, 'wide', axis=0, tiled=True)  124 us
    all_gather x1, waiting for transfers between devices, on_device(): weight_panel = lax.all_gather(down_weight, 'narrow', axis=0, tiled=True)  81.4 us
    dot_general x1, matrix products, on_device(): jnp.dot(weight_panel, lax.all_gather(rot_half, 'wide', axis=0, tiled=True...  51.8 us
    reduce_scatter x1, waiting for transfers between devices, on_device(): lax.psum_scatter(jnp.dot(quantized, both_weights, preferred_element_type=...  40.3 us
    all_gather x1, blocking collectives, on_device(): target_rows = lax.all_gather(cotangent, 'wide', axis=0, tiled=True)  19.9 us
    psum x1, waiting for transfers between devices, on_device(): lax.psum(part_proj.astype(jnp.bfloat16), 'narrow').astype(jnp.float32)  16.3 us
    reduce_sum x1, other arithmetic, on_device(): applied = shards.sum(axis=0)  13.1 us
  transfers between devices with their start and end apart: 7, of which 6 were waited for; matrix products, arithmetic and copies ran while one was open for 12% of the time, Pallas kernels for 0%

profile of v1, /device:TPU:0, one launch (start us, length us, event | category | flops | bytes accessed | tf_op | source)
XLA Modules:
  0.0 596.0 jit_solution(13270391516895125776)
XLA Ops:
  7.2 0.0 copy-start
  7.2 0.0 copy-start.4
  7.2 0.0 copy-start.2
  7.2 0.0 all-gather.5.cloned.1.call-start
  7.2 0.7 all-gather.5.cloned.1.call-update
  7.9 0.0 all-gather.7.cloned.1.call-start
  8.0 0.8 copy-done
  8.8 1.1 convert_element_type.49
  9.9 0.0 copy-start.6
  9.9 0.0 copy-start.5
  9.9 0.0 all-gather.7.cloned.1.call-update
  9.9 0.0 copy-done.4
  9.9 0.0 copy-done.2
  10.0 0.4 fusion.14
  10.4 0.4 convolution_bitcast_fusion
  10.8 0.2 copy.23
  11.0 10.0 %all_gather.21 = f32[8,16384]{1,0:T(8,128)S(1)} all-gather(f32[8,8192]{1,0:T(8,128)S(1)} %bitcast.44), channel_id=1, replica_groups=mesh['wide'=16,'narrow'=2] {'narrow'}, dimensions={1}, use_global_device_ids=true | all-gather | bytes 786432 | tf_op jit(solution)/shard_map/all_gather | solution.py:49
  20.9 0.5 reshape.43
  21.4 2.7 fusion
  24.1 1.6 div.38
  25.7 0.0 copy-done.6
  25.7 2.8 multiply_convert_fusion.1
  28.5 6.1 %all-to-all-start = ((bf16[8,16,1024]{2,0,1:T(8,128)(2,1)}), bf16[8,16,1024]{2,0,1:T(8,128)(2,1)S(1)}, u32[]{:S(2)}, u32[]{:S(2)}) async-start(bf16[8,16,1024]{2,0,1:T(8,128)(2,1)} %multiply_convert_fusion.1), calls=%async_computation | async-start | bytes 524288 | tf_op jit(solution)/shard_map/all_to_all | solution.py:55
  34.6 0.2 reduce-scatter.2.cloned.1.call-start
  34.9 0.0 copy-done.5
  34.9 81.4 %all-gather.5.cloned.1.call-done = bf16[1024,4096]{1,0:T(8,128)(2,1)} async-done(((bf16[512,4096]{1,0:T(8,128)(2,1)}), bf16[1024,4096]{1,0:T(8,128)(2,1)}) %all-gather.5.cloned.1.call-update) | async-done | bytes 8388624 | tf_op jit(solution)/shard_map/all_gather | solution.py:56
  116.3 4.7 constant_dynamic-slice_fusion
  121.0 124.5 %all-gather.7.cloned.1.call-done = bf16[4096,2048]{1,0:T(8,128)(2,1)} async-done(((bf16[256,2048]{1,0:T(8,128)(2,1)}), bf16[4096,2048]{1,0:T(8,128)(2,1)}) %all-gather.7.cloned.1.call-update) | async-done | bytes 16777232 | tf_op jit(solution)/shard_map/all_gather | solution.py:61
  245.5 51.8 %multiply_convert_fusion = bf16[1024,2048]{1,0:T(8,128)(2,1)} fusion(bf16[1024,4096]{1,0:T(8,128)(2,1)} %all-gather.5.cloned.1.call-done, bf16[4096,2048]{1,0:T(8,128)(2,1)} %all-gather.7.cloned.1.call-done, f32[2048]{0:T(1024)S(1)} %multiply_exponential_fusion), kind=kOutput, calls=%fused_computation.6 | convolution fusion | flops 17196646400 | bytes 29368320 | tf_op jit(solution)/shard_map/dot_general | solution.py:59
  297.2 0.0 copy-start.3
  297.2 0.0 all-to-all-done
  297.2 5.5 fusion.1
  302.8 0.0 reduce-scatter.2.cloned.1.call-update
  302.8 0.0 copy-done.3
  302.8 19.9 %all_gather.25 = bf16[128,2048]{1,0:T(8,128)(2,1)S(1)} all-gather(bf16[8,2048]{1,0:T(8,128)(2,1)S(1)} %copy-done.3), channel_id=1, replica_groups=mesh['wide'=16,'narrow'=2] {'wide'}, dimensions={0}, use_global_device_ids=true | all-gather | bytes 557056 | tf_op jit(solution)/shard_map/all_gather | solution.py:76
  322.7 40.3 %reduce-scatter.2.cloned.1.call-done = f32[8,4096]{1,0:T(8,128)} async-done(((f32[128,4096]{1,0:T(8,128)}), f32[8,4096]{1,0:T(8,128)}) %reduce-scatter.2.cloned.1.call-update) | async-done | bytes 131088 | tf_op jit(solution)/shard_map/reduce_scatter | solution.py:68
  362.9 0.9 convert.5
  363.9 0.6 fusion.85
  364.5 4.7 all_gather.24
  369.2 3.7 all-to-all-start.1
  372.8 0.3 all-reduce.2.cloned.1.call-start
  373.1 1.9 convolution_convert_fusion
  375.0 0.0 all-reduce.2.cloned.1.call-update
  375.0 0.0 all-gather.9.cloned.1.call-start
  375.7 4.0 all-to-all-done.1
  379.7 1.8 subtract_add_fusion
  381.5 16.3 %all-reduce.2.cloned.1.call-done = bf16[128,256]{1,0:T(8,128)(2,1)} async-done(((bf16[128,256]{1,0:T(8,128)(2,1)}), bf16[128,256]{1,0:T(8,128)(2,1)}) %all-reduce.2.cloned.1.call-update) | async-done | bytes 65552 | tf_op jit(solution)/shard_map/psum | solution.py:84
  397.8 4.1 fusion.16
  402.0 0.0 all-gather.9.cloned.1.call-update
  402.0 168.2 %all-gather.9.cloned.1.call-done = f32[4096,2048]{1,0:T(8,128)} async-done(((f32[256,2048]{1,0:T(8,128)}), f32[4096,2048]{1,0:T(8,128)}) %all-gather.9.cloned.1.call-update) | async-done | bytes 33554448 | tf_op jit(solution)/shard_map/all_gather | solution.py:89
  570.2 0.0 copy-start.1
  570.2 13.1 %reduce_sum.9 = f32[256,2048]{1,0:T(8,128)} reduce(f32[16,256,2048]{2,1,0:T(8,128)} %bitcast.42, f32[]{:T(128)} %constant.86.clone.1), dimensions={0}, to_apply=%region_2.3 | reduce | flops 7864320 | bytes 35651588 | tf_op jit(solution)/shard_map/reduce_sum | solution.py:90
  583.3 2.2 fusion.9
  585.5 0.0 copy-done.1
  585.6 3.9 fusion.7
  (4 shorter events, 0.0 us)
Async XLA Ops:
  7.2 1.6 copy-start
  7.2 2.7 copy-start.4
  7.2 2.8 copy-start.2
  7.2 109.1 %all-gather.5.cloned.1.call-start = ((), (), s32[]{:S(2)}) async-start(), calls=%async_computation.3 | async-start | bytes 12582912 | tf_op jit(solution)/shard_map/all_gather | solution.py:56
  7.9 237.5 %all-gather.7.cloned.1.call-start = ((), (), s32[]{:S(2)}) async-start(), calls=%async_computation.4 | async-start | bytes 17825792 | tf_op jit(solution)/shard_map/all_gather | solution.py:61
  9.9 15.8 %copy-start.6 = (s32[8]{0:T(128)S(1)}, s32[8]{0:T(128)}, u32[]{:S(2)}) copy-start(s32[8]{0:T(128)} %param.12) | copy-start | bytes 100
  9.9 25.0 %copy-start.5 = (s32[2048]{0:T(1024)S(1)}, s32[2048]{0:T(1024)}, u32[]{:S(2)}) copy-start(s32[2048]{0:T(1024)} %param.13) | copy-start | bytes 24580
  28.5 268.8 %all-to-all-start = ((bf16[8,16,1024]{2,0,1:T(8,128)(2,1)}), bf16[8,16,1024]{2,0,1:T(8,128)(2,1)S(1)}, u32[]{:S(2)}, u32[]{:S(2)}) async-start(bf16[8,16,1024]{2,0,1:T(8,128)(2,1)} %multiply_convert_fusion.1), calls=%async_computation | async-start | bytes 524288 | tf_op jit(solution)/shard_map/all_to_all | solution.py:55
  34.6 328.3 %reduce-scatter.2.cloned.1.call-start = ((), (), s32[]{:S(2)}) async-start(), calls=%async_computation.5 | async-start | bytes 2228224 | tf_op jit(solution)/shard_map/reduce_scatter | solution.py:68
  297.2 5.6 copy-start.3
  369.2 10.6 %all-to-all-start.1 = ((bf16[8,16,256]{2,0,1:T(8,128)(2,1)}), bf16[8,16,256]{2,0,1:T(8,128)(2,1)S(1)}, u32[]{:S(2)}, u32[]{:S(2)}) async-start(bf16[8,16,256]{2,0,1:T(8,128)(2,1)} %bitcast.8), calls=%async_computation.2 | async-start | bytes 131072 | tf_op jit(solution)/shard_map/all_to_all | solution.py:78
  372.8 25.0 %all-reduce.2.cloned.1.call-start = ((), (), s32[]{:S(2)}) async-start(), calls=%async_computation.6 | async-start | bytes 131072 | tf_op jit(solution)/shard_map/psum | solution.py:84
  375.0 195.1 %all-gather.9.cloned.1.call-start = ((), (), s32[]{:S(2)}) async-start(), calls=%async_computation.7 | async-start | bytes 35651584 | tf_op jit(solution)/shard_map/all_gather | solution.py:89
  570.2 15.4 %copy-start.1 = (bf16[128,256]{1,0:T(8,128)(2,1)S(1)}, bf16[128,256]{1,0:T(8,128)(2,1)}, u32[]{:S(2)}) copy-start(bf16[128,256]{1,0:T(8,128)(2,1)} %all-reduce.2.cloned.1.call-done) | copy-start | bytes 196612
Sparse Core Ops, SparseCore 0:
  9.5 106.6 all-gather.4
  119.0 126.4 all-gather.6
  302.9 59.9 reduce-scatter.1
  375.6 22.2 all-reduce.1
  402.1 168.0 all-gather.8
